TPU v7x, 512 devices: a whole 4x8x8 slice. The times are simulated.
512 devices in a mesh: ind: 32 (over z, x), snp: 16 (over y, core).
Axes of the slice: x: 4, y: 8, z: 8, core: 2. Of those that a mesh axis runs over, the one named last changes fastest.
Arguments:
- genotype: int32 [16384, 32768], P('ind', 'snp'), may hold values from 0 to 170, as said below
- probe: bfloat16 [24, 32768], P(None, 'snp'), may hold values from -0.03125 to 0.03125
- allele_mean: float32 [32768], P('snp'), may hold values from 0.2 to 1.8
- allele_scale: float32 [32768], P('snp'), may hold values from 0.3 to 3
Outputs:
- projected: float32 [24, 32768], P(None, 'snp')
Inputs may be any that keep to these rules, and one draw needn't show every extreme that they name: `genotype`: word r of a column holds the codes of individuals 4 r + k, k = 0 to 3, in bits 2 k and 2 k + 1; every code is 0, 1 or 2.
All inputs are finite; a program needn't handle non-finite values.
Results may differ from a plain program's by a relative error of at most 0.0095.
Values may be sent and summed in bfloat16 or wider, within the bound.
No kernel may reach another device: no remote copies, remote signals or barrier semaphores. Data moves between devices by JAX's collectives and lax.ppermute only.
A program may use at most 64 MiB of HBM per device.

v0:
```python
import math

import jax
import jax.numpy as jnp
from jax import lax
from jax.sharding import PartitionSpec as P


def unpack(packed, allele_mean, allele_scale):
    planes = []
    for offset in range(4):
        codes = jnp.bitwise_and(jnp.right_shift(packed, 2 * offset), 3)
        planes.append(
            ((codes.astype(jnp.float32) - allele_mean) * allele_scale).astype(jnp.bfloat16)
        )
    stacked = jnp.stack(planes, axis=1)
    return stacked.reshape(packed.shape[0] * 4, packed.shape[1])


def sketch_rows(genotype, probe, allele_mean, allele_scale):
    word_rows = genotype.shape[0]
    block_words = math.gcd(word_rows, 32)
    blocks = genotype.reshape(word_rows // block_words, block_words, genotype.shape[1])

    def one_block(packed):
        zed = unpack(packed, allele_mean, allele_scale)
        return lax.dot_general(
            probe, zed, (((1,), (1,)), ((), ())), preferred_element_type=jnp.float32
        )

    pieces = lax.map(one_block, blocks)
    return pieces.transpose(1, 0, 2).reshape(probe.shape[0], word_rows * 4)


def project_rows(packed_rows, basis_cols, allele_mean, allele_scale):
    word_rows = packed_rows.shape[0]
    block_words = math.gcd(word_rows, 32)
    block_count = word_rows // block_words
    blocks = packed_rows.reshape(block_count, block_words, packed_rows.shape[1])
    basis_blocks = basis_cols.reshape(basis_cols.shape[0], block_count, 4 * block_words).transpose(
        1, 0, 2
    )

    def step_block(total, inputs):
        packed, basis_block = inputs
        zed = unpack(packed, allele_mean, allele_scale)
        return (total + jnp.dot(basis_block, zed, preferred_element_type=jnp.float32), 0.0)

    start_total = jnp.zeros((basis_cols.shape[0], packed_rows.shape[1]), jnp.float32)
    total, ignored = lax.scan(step_block, start_total, (blocks, basis_blocks))
    return total


def on_device(genotype, probe, allele_mean, allele_scale):
    partial_sketch = sketch_rows(genotype, probe, allele_mean, allele_scale)
    share = partial_sketch.shape[1] // lax.axis_size("snp")
    sketch = lax.psum(partial_sketch.astype(jnp.bfloat16), "snp").astype(jnp.float32)
    slice_rows = lax.dynamic_slice_in_dim(sketch, lax.axis_index("snp") * share, share, 1)
    gram = jnp.dot(
        slice_rows,
        slice_rows.T,
        precision=lax.Precision.HIGHEST,
        preferred_element_type=jnp.float32,
    )
    total = lax.psum(gram, ("ind", "snp"))
    lower = jnp.linalg.cholesky(total)
    basis = jax.scipy.linalg.solve_triangular(lower, sketch, lower=True).astype(jnp.bfloat16)
    product = project_rows(genotype, basis, allele_mean, allele_scale)
    return lax.psum(product.astype(jnp.bfloat16), "ind").astype(jnp.float32)


def solution(mesh):
    in_specs = (P("ind", "snp"), P(None, "snp"), P("snp"), P("snp"))
    out_specs = P(None, "snp")
    return jax.shard_map(
        on_device, mesh=mesh, in_specs=in_specs, out_specs=out_specs, check_vma=False
    )
```

profile of v0, /device:TPU:1, one launch (start us, length us, event | category | flops | bytes accessed | tf_op | source)
XLA Modules:
  0.0 548.6 jit_solution(3757689987659371979)
XLA Ops:
  6.5 6.6 %copy.12 = s32[16,32,2048]{2,0,1:T(8,128)} copy(s32[16,32,2048]{2,1,0:T(8,128)} %bitcast.101) | data formatting | bytes 8388608 | tf_op jit(solution)/shard_map/while | solution.py:31
  13.1 78.9 %while.21 = (s32[]{:T(128)}, bf16[16,24,128]{2,1,0:T(8,128)(2,1)S(1)}, s32[16,32,2048]{2,0,1:T(8,128)}, f32[2048]{0:T(1024)S(1)}, f32[2048]{0:T(1024)S(1)}, /*index=5*/bf16[24,2048]{1,0:T(8,128)(2,1)S(1)}, s32[]{:T(128)}) while((s32[]{:T(128)}, bf16[16,24,128]{2,1,0:T(8,128)(2,1)S(1)}, s32[16,32,2048]{2,0,1:T(8,128)}, f32[2048]{0:T(1024)S(1)}, ...), condition=%wide.region_1.2_spmd, body=%wide.region_0.1_spmd.sunk | while | flops 16252930 | bytes 3534933 | solution.py:31
  13.1 3.3 fusion.41
  16.5 1.2 pad_maximum_fusion.4
  18.1 3.3 fusion.41
  23.0 3.3 fusion.41
  27.9 3.3 fusion.41
  32.9 3.3 fusion.41
  37.8 3.3 fusion.41
  41.1 1.2 pad_maximum_fusion.4
  42.7 3.3 fusion.41
  46.1 1.2 pad_maximum_fusion.4
  47.7 3.3 fusion.41
  52.6 3.3 fusion.41
  55.9 1.2 pad_maximum_fusion.4
  57.5 3.3 fusion.41
  60.9 1.2 pad_maximum_fusion.4
  62.5 3.3 fusion.41
  65.8 1.2 pad_maximum_fusion.4
  67.4 3.3 fusion.41
  70.7 1.2 pad_maximum_fusion.4
  72.3 3.3 fusion.41
  77.3 3.3 fusion.41
  82.2 3.3 fusion.41
  87.1 3.3 fusion.41
  92.8 116.7 %all-reduce.3.cloned.1.call-done = bf16[24,2048]{1,0:T(8,128)(2,1)} async-done(((bf16[24,2048]{1,0:T(8,128)(2,1)}), bf16[24,2048]{1,0:T(8,128)(2,1)}) %all-reduce.3.cloned.1.call-update) | async-done | bytes 98320 | tf_op jit(solution)/shard_map/psum | solution.py:57
  210.4 98.0 %psum.22 = f32[24,24]{0,1:T(8,128)S(1)} all-reduce(f32[24,24]{0,1:T(8,128)S(1)} %fusion.24), channel_id=1, replica_groups=mesh['ind'=32,'snp'=16] {'ind','snp'}, use_global_device_ids=true, to_apply=%region_3.4 | all-reduce | flops 576 | bytes 4608 | tf_op jit(solution)/shard_map/psum | solution.py:65
  308.4 2.2 cholesky.16
  312.0 1.8 custom-call.7
  315.0 78.2 %while.22 = (s32[]{:T(128)}, f32[24,2048]{1,0:T(8,128)S(1)}, bf16[16,24,128]{2,1,0:T(8,128)(2,1)S(1)}, s32[16,32,2048]{2,0,1:T(8,128)}, f32[2048]{0:T(1024)S(1)}, /*index=5*/f32[2048]{0:T(1024)S(1)}, s32[]{:T(128)}, s32[]{:T(128)}) while((s32[]{:T(128)}, f32[24,2048]{1,0:T(8,128)S(1)}, bf16[16,24,128]{2,1,0:T(8,128)(2,1)S(1)}, ...), condition=%wide.region_7.8_spmd.clone, body=%wide.region_6.7_spmd.clone.sunk | while | flops 16351235 | bytes 3823719 | solution.py:50
  315.0 3.3 fusion.45
  319.9 3.3 fusion.45
  324.8 3.3 fusion.45
  329.7 3.3 fusion.45
  334.6 3.3 fusion.45
  339.5 3.3 fusion.45
  344.4 3.3 fusion.45
  349.2 3.3 fusion.45
  354.1 3.3 fusion.45
  359.0 3.3 fusion.45
  363.9 3.3 fusion.45
  368.8 3.3 fusion.45
  373.7 3.3 fusion.45
  378.6 3.3 fusion.45
  383.5 3.3 fusion.45
  388.3 3.3 fusion.45
  393.9 146.3 %all-reduce.5.cloned.1.call-done = bf16[24,2048]{1,0:T(8,128)(2,1)} async-done(((bf16[24,2048]{1,0:T(8,128)(2,1)}), bf16[24,2048]{1,0:T(8,128)(2,1)}) %all-reduce.5.cloned.1.call-update) | async-done | bytes 98320 | tf_op jit(solution)/shard_map/psum | solution.py:69
  540.2 1.6 convert_element_type.208
  (111 shorter events, 46.6 us)
Async XLA Ops:
  6.5 203.0 %all-reduce.3.cloned.1.call-start = ((), (), s32[]{:S(2)}) async-start(), calls=%async_computation | async-start | bytes 196608 | tf_op jit(solution)/shard_map/psum | solution.py:57
  6.5 6.6 %copy-start = (bf16[24,2048]{1,0:T(8,128)(2,1)S(1)}, bf16[24,2048]{1,0:T(8,128)(2,1)}, u32[]{:S(2)}) copy-start(bf16[24,2048]{1,0:T(8,128)(2,1)} %param.9) | copy-start | bytes 294916
  6.5 6.6 %copy-start.1 = (f32[2048]{0:T(1024)S(1)}, f32[2048]{0:T(1024)}, u32[]{:S(2)}) copy-start(f32[2048]{0:T(1024)} %param.10) | copy-start | bytes 24580
  6.5 6.6 %copy-start.2 = (f32[2048]{0:T(1024)S(1)}, f32[2048]{0:T(1024)}, u32[]{:S(2)}) copy-start(f32[2048]{0:T(1024)} %param.11) | copy-start | bytes 24580
  92.8 447.4 %all-reduce.5.cloned.1.call-start = ((), (), s32[]{:S(2)}) async-start(), calls=%async_computation.1 | async-start | bytes 196608 | tf_op jit(solution)/shard_map/psum | solution.py:69
Sparse Core Ops, SparseCore 0:
  92.9 116.5 all-reduce.2
  394.0 146.1 all-reduce.4
where the time goes:
time: 553 us; the launch traced here: 549 us
  waiting for transfers between devices  263 us (48%)
  other arithmetic  153 us (28%)
  blocking collectives  98 us (18%)
  between operations  13.5 us (2%)
  local copies, waits for them, and re-layouts  11.2 us (2%)
  matrix products  9.34 us (2%)
    psum x1, waiting for transfers between devices, on_device(): return lax.psum(product.astype(jnp.bfloat16), 'ind').astype(jnp.float32)  146 us
    psum x1, waiting for transfers between devices, on_device(): lax.psum(partial_sketch.astype(jnp.bfloat16), 'snp').astype(jnp.float32)  117 us
    convert_element_type x32, other arithmetic, unpack(): ((codes.astype(jnp.float32) - allele_mean) * allele_scale).astype(jnp.bfl...  106 us
    psum x1, blocking collectives, on_device(): total = lax.psum(gram, ('ind', 'snp'))  98 us
    another operation x32, other arithmetic, unpack(): stacked = jnp.stack(planes, axis=1)  39.1 us
  transfers between devices with their start and end apart: 2, of which 2 were waited for; matrix products, arithmetic and copies ran while one was open for 0% of the time, Pallas kernels for 0%

commit v1 on v0

v1 whole, which is shorter than its diff:
```python
import jax
import jax.numpy as jnp
from jax import lax
from jax.experimental import pallas as pl
from jax.experimental.pallas import tpu as pltpu
from jax.sharding import PartitionSpec as P

F32, BF16 = jnp.float32, jnp.bfloat16
NT = (((1,), (1,)), ((), ()))
LANES = 128


def digits(words):
    return jnp.concatenate(
        [jnp.bitwise_and(words, 3 << (2 * p)).astype(F32).astype(BF16) for p in range(4)],
        axis=0,
    )


def sketch_kernel(words_ref, probe_ref, mean_ref, scale_ref, out_ref, weight_ref, shift_ref):
    rank = probe_ref.shape[0]
    step = pl.program_id(0)
    steps = pl.num_programs(0)

    @pl.when(step == 0)
    def _():
        weight = probe_ref[...].astype(F32) * scale_ref[...]
        high = weight.astype(BF16)
        weight_ref[0:rank, :] = high.astype(F32)
        weight_ref[rank : 2 * rank, :] = weight - high.astype(F32)
        shift = jnp.sum(weight * mean_ref[...], axis=1, keepdims=True)
        shift_ref[...] = jnp.broadcast_to(shift, shift_ref.shape)

    rows = words_ref.shape[0]
    both = lax.dot_general(
        digits(words_ref[...]), weight_ref[...].astype(BF16), NT, preferred_element_type=F32
    )
    for p in range(4):
        part = both[p * rows : (p + 1) * rows, :].T
        total = (part[0:rank, :] + part[rank : 2 * rank, :]) * (0.25**p)
        out_ref[p * steps + step] = (total - shift_ref[...]).astype(BF16)


def sketch_partial(genotype, probe, mean, scale):
    words, snps = genotype.shape
    rank = probe.shape[0]
    steps = words // LANES
    whole = lambda g: (0, 0)
    return pl.pallas_call(
        sketch_kernel,
        grid=(steps,),
        in_specs=[
            pl.BlockSpec((LANES, snps), lambda g: (g, 0)),
            pl.BlockSpec((rank, snps), whole),
            pl.BlockSpec((1, snps), whole),
            pl.BlockSpec((1, snps), whole),
        ],
        out_specs=pl.BlockSpec((4 * steps, rank, LANES), lambda g: (0, 0, 0)),
        out_shape=jax.ShapeDtypeStruct((4 * steps, rank, LANES), BF16),
        scratch_shapes=[pltpu.VMEM((2 * rank, snps), F32), pltpu.VMEM((rank, LANES), F32)],
        name="sketch",
    )(genotype, probe, mean, scale)


def gather_kernel(parts_ref, out_ref):
    total = parts_ref[0].astype(F32)
    for source in range(1, parts_ref.shape[0]):
        total = total + parts_ref[source].astype(F32)
    chunk = total.astype(BF16)
    for target in range(out_ref.shape[0]):
        out_ref[target] = chunk


def sum_and_copy(parts):
    return pl.pallas_call(
        gather_kernel, out_shape=jax.ShapeDtypeStruct(parts.shape, BF16), name="sumsnp"
    )(parts)


def project_kernel(words_ref, sketch_ref, mean_ref, scale_ref, out_ref, total_ref):
    chunks, rank, width = sketch_ref.shape
    step = pl.program_id(0)
    steps = pl.num_programs(0)
    left = jnp.concatenate(
        [sketch_ref[p * steps + step].astype(F32) * (0.25**p) for p in range(4)], axis=1
    ).astype(BF16)
    piece = jnp.dot(left, digits(words_ref[...]), preferred_element_type=F32)

    @pl.when(step == 0)
    def _():
        total_ref[...] = piece

    @pl.when(step > 0)
    def _():
        total_ref[...] += piece

    @pl.when(step == steps - 1)
    def _():
        gram = jnp.zeros((rank, rank), F32)
        sums = jnp.zeros((rank, width), F32)
        for b in range(chunks):
            block = sketch_ref[b]
            gram = gram + lax.dot_general(block, block, NT, preferred_element_type=F32)
            sums = sums + block.astype(F32)
        sums = jnp.sum(sums, axis=1, keepdims=True)
        half = width // 2
        side = jnp.concatenate(
            [jnp.zeros((rank, half), F32), gram, jnp.zeros((rank, half - rank), F32)], axis=1
        )
        low = lax.broadcasted_iota(jnp.int32, (rank, width), 1) < half
        for c in range(total_ref.shape[1] // width):
            cols = slice(c * width, (c + 1) * width)
            block = (total_ref[:, cols] - mean_ref[:, cols] * sums) * scale_ref[:, cols]
            out_ref[2 * c] = jnp.where(low, block, side)
            out_ref[2 * c + 1] = jnp.where(low, pltpu.roll(block, half, 1), side)


def project_partial(genotype, sketch, mean, scale):
    words, snps = genotype.shape
    chunks, rank, width = sketch.shape
    steps = words // width
    whole = lambda g: (0, 0)
    shape = (2 * snps // width, rank, width)
    return pl.pallas_call(
        project_kernel,
        grid=(steps,),
        in_specs=[
            pl.BlockSpec((width, snps), lambda g: (g, 0)),
            pl.BlockSpec(sketch.shape, lambda g: (0, 0, 0)),
            pl.BlockSpec((1, snps), whole),
            pl.BlockSpec((1, snps), whole),
        ],
        out_specs=pl.BlockSpec(shape, lambda g: (0, 0, 0)),
        out_shape=jax.ShapeDtypeStruct(shape, F32),
        scratch_shapes=[pltpu.VMEM((rank, snps), F32)],
        name="project",
    )(genotype, sketch, mean, scale)


def solve_kernel(parts_ref, out_ref):
    sources, rank, width = parts_ref.shape
    half = width // 2
    work = parts_ref[0]
    for source in range(1, sources):
        work = work + parts_ref[source]
    row = lax.broadcasted_iota(jnp.int32, (rank, width), 0)
    scales = jnp.zeros((rank, 1), F32)
    for k in range(rank):
        pivot_row = work[k : k + 1, :]
        column = work[:, half + k : half + k + 1]
        pivot = work[k : k + 1, half + k : half + k + 1]
        scales = jnp.where(row[:, 0:1] == k, lax.rsqrt(pivot), scales)
        factor = jnp.where(row[:, 0:1] > k, column / pivot, 0.0)
        work = work - factor * pivot_row
    chunk = (work * scales).astype(BF16)
    for target in range(out_ref.shape[0]):
        out_ref[target] = chunk


def solve(parts):
    return pl.pallas_call(
        solve_kernel, out_shape=jax.ShapeDtypeStruct(parts.shape, BF16), name="solve"
    )(parts)


def finish_kernel(parts_ref, out_ref):
    chunks, rank, width = parts_ref.shape
    half = width // 2
    low = lax.broadcasted_iota(jnp.int32, (rank, width), 1) < half
    for c in range(chunks // 2):
        first = parts_ref[2 * c].astype(F32)
        second = pltpu.roll(parts_ref[2 * c + 1].astype(F32), half, 1)
        out_ref[:, c * width : (c + 1) * width] = jnp.where(low, first, second)


def finish(parts):
    chunks, rank, width = parts.shape
    return pl.pallas_call(
        finish_kernel,
        out_shape=jax.ShapeDtypeStruct((rank, chunks * width // 2), F32),
        name="finish",
    )(parts)


def exchange(chunks, axis):
    return lax.all_to_all(chunks, axis, 0, 0, tiled=True)


def on_device(genotype, probe, allele_mean, allele_scale):
    mean, scale = allele_mean[None, :], allele_scale[None, :]
    parts = exchange(sketch_partial(genotype, probe, mean, scale), "snp")
    sketch = exchange(sum_and_copy(parts), "snp")
    parts = exchange(project_partial(genotype, sketch, mean, scale), "ind")
    return finish(exchange(solve(parts), "ind"))


def solution(mesh):
    in_specs = (P("ind", "snp"), P(None, "snp"), P("snp"), P("snp"))
    return jax.shard_map(
        on_device, mesh=mesh, in_specs=in_specs, out_specs=P(None, "snp"), check_vma=False
    )
```

time: 553 us -> 90.3 us (0.16)
  waiting for transfers between devices: 263 us -> 0 us
  other arithmetic: 153 us -> 0 us
  blocking collectives: 98 us -> 71.5 us
  Pallas kernels: 0 us -> 17.7 us
  between operations: 13.5 us -> 0.01 us
  local copies, waits for them, and re-layouts: 11.2 us -> 0 us
  matrix products: 9.34 us -> 0 us
    psum x2 -> x0, waiting for transfers between devices: 263 us -> none  [the longest x1 146 us: on_device(): return lax.psum(product.astype(jnp.bfloat16), 'ind').astype(jnp.float32)]
    convert_element_type x34 -> x0, other arithmetic: 108 us -> none  [the longest x32 106 us: unpack(): ((codes.astype(jnp.float32) - allele_mean) * allele_scale).astype(jnp.bfl...]
    psum x1 -> x0, blocking collectives: 98 us -> none  [on_device(): total = lax.psum(gram, ('ind', 'snp'))]
    all_to_all x0 -> x4, blocking collectives: none -> 71.5 us  [exchange(): return lax.all_to_all(chunks, axis, 0, 0, tiled=True)]
    another operation x37 -> x0, other arithmetic: 44.5 us -> none  [the longest x32 39.1 us: unpack(): stacked = jnp.stack(planes, axis=1)]
    pallas_call x0 -> x5, Pallas kernels: none -> 17.7 us  [the longest x1 5.52 us: sketch_partial(): pl.pallas_call(sketch_kernel, grid=(steps,), in_specs=[pl.BlockSpec((LANE...]
    dot_general x33 -> x0, matrix products: 8.14 us -> none  [the longest x16 4.13 us: one_block(): lax.dot_general(probe, zed, (((1,), (1,)), ((), ())), preferred_element_t...]
    while x1 -> x0, local copies, waits for them, and re-layouts: 6.58 us -> none  [sketch_rows(): pieces = lax.map(one_block, blocks)]
  transfers between devices with their start and end apart: 2 -> 0, of which waited for: 2 -> 0; matrix products, arithmetic and copies ran while one was open for 0% -> 0% of each run, Pallas kernels for 0% -> 0%
where the time goes in v1:
time: 90.3 us; the launch traced here: 89.2 us
  blocking collectives  71.5 us (79%)
  Pallas kernels  17.7 us (20%)
    all_to_all x4, blocking collectives, exchange(): return lax.all_to_all(chunks, axis, 0, 0, tiled=True)  71.5 us
    pallas_call x1, Pallas kernels, sketch_partial(): pl.pallas_call(sketch_kernel, grid=(steps,), in_specs=[pl.BlockSpec((LANE...  5.52 us
    pallas_call x1, Pallas kernels, project_partial(): pl.pallas_call(project_kernel, grid=(steps,), in_specs=[pl.BlockSpec((wid...  5.2 us
    pallas_call x1, Pallas kernels, solve(): pl.pallas_call(solve_kernel, out_shape=jax.ShapeDtypeStruct(parts.shape,...  3.71 us

profile of v1, /device:TPU:1, one launch (start us, length us, event | category | flops | bytes accessed | tf_op | source)
XLA Modules:
  0.0 89.2 jit_solution(7708085008271294255)
XLA Ops:
  0.0 5.5 %sketch.1 = bf16[16,24,128]{2,1,0:T(8,128)(2,1)} custom-call(s32[512,2048]{1,0:T(8,128)} %words_ref.3, bf16[24,2048]{1,0:T(8,128)(2,1)} %probe_ref.1, f32[1,2048]{1,0:T(1,128)} %bitcast.2, f32[1,2048]{1,0:T(1,128)} %bitcast.4), custom_call_target="tpu_custom_call" | custom-call | tf_op jit(solution)/shard_map/sketch/pallas_call | solution.py:49
  5.5 19.3 %all_to_all.20.parts_ref = bf16[16,24,128]{2,1,0:T(8,128)(2,1)} all-to-all(bf16[16,24,128]{2,1,0:T(8,128)(2,1)} %sketch.1), channel_id=1, replica_groups=mesh['ind'=32,'snp'=16] {'snp'}, dimensions={0} | all-to-all | bytes 196608 | tf_op jit(solution)/shard_map/all_to_all | solution.py:186
  24.8 1.6 %sumsnp.1 = bf16[16,24,128]{2,1,0:T(8,128)(2,1)} custom-call(bf16[16,24,128]{2,1,0:T(8,128)(2,1)} %all_to_all.20.parts_ref), custom_call_target="tpu_custom_call" | custom-call | tf_op jit(solution)/shard_map/sumsnp/pallas_call | solution.py:75
  26.4 12.4 %all_to_all.21.sketch_ref = bf16[16,24,128]{2,1,0:T(8,128)(2,1)} all-to-all(bf16[16,24,128]{2,1,0:T(8,128)(2,1)} %sumsnp.1), channel_id=1, replica_groups=mesh['ind'=32,'snp'=16] {'snp'}, dimensions={0} | all-to-all | bytes 196608 | tf_op jit(solution)/shard_map/all_to_all | solution.py:186
  38.8 5.2 %project.1 = f32[32,24,128]{2,1,0:T(8,128)} custom-call(s32[512,2048]{1,0:T(8,128)} %words_ref.3, bf16[16,24,128]{2,1,0:T(8,128)(2,1)} %all_to_all.21.sketch_ref, f32[1,2048]{1,0:T(1,128)} %bitcast.3, f32[1,2048]{1,0:T(1,128)} %bitcast.5), custom_call_target="tpu_custom_call" | custom-call | tf_op jit(solution)/shard_map/project/pallas_call | solution.py:124
  44.0 25.3 %all_to_all.22.parts_ref = f32[32,24,128]{2,1,0:T(8,128)} all-to-all(f32[32,24,128]{2,1,0:T(8,128)} %project.1), channel_id=1, replica_groups=mesh['ind'=32,'snp'=16] {'ind'}, dimensions={0} | all-to-all | bytes 786432 | tf_op jit(solution)/shard_map/all_to_all | solution.py:186
  69.4 3.7 %solve.1 = bf16[32,24,128]{2,1,0:T(8,128)(2,1)} custom-call(f32[32,24,128]{2,1,0:T(8,128)} %all_to_all.22.parts_ref), custom_call_target="tpu_custom_call" | custom-call | tf_op jit(solution)/shard_map/solve/pallas_call | solution.py:161
  73.1 14.4 %all_to_all.23.parts_ref = bf16[32,24,128]{2,1,0:T(8,128)(2,1)} all-to-all(bf16[32,24,128]{2,1,0:T(8,128)(2,1)} %solve.1), channel_id=1, replica_groups=mesh['ind'=32,'snp'=16] {'ind'}, dimensions={0} | all-to-all | bytes 393216 | tf_op jit(solution)/shard_map/all_to_all | solution.py:186
  87.5 1.7 %finish.1 = f32[24,2048]{1,0:T(8,128)} custom-call(bf16[32,24,128]{2,1,0:T(8,128)(2,1)} %all_to_all.23.parts_ref), custom_call_target="tpu_custom_call" | custom-call | tf_op jit(solution)/shard_map/finish/pallas_call | solution.py:178

commit v2 on v0

v2 whole, which is shorter than its diff:
```python
import functools

import jax
import jax.numpy as jnp
from jax import lax
from jax.experimental import pallas as pl
from jax.experimental.pallas import tpu as pltpu
from jax.sharding import PartitionSpec as P

F32, BF16 = jnp.float32, jnp.bfloat16
NT = (((1,), (1,)), ((), ()))
LANES = 128
HALF = 64
HBM = pl.BlockSpec(memory_space=pltpu.HBM)
VMEM = pl.BlockSpec(memory_space=pltpu.VMEM)


def params(mib):
    return pltpu.CompilerParams(vmem_limit_bytes=mib << 20)


def sketch_kernel(
    words_hbm, probe_hbm, mean_hbm, scale_hbm, out_ref, digits_ref, mean_ref, scale_ref,
    words, probe_ref, small_sems, big_sems,
):
    rank = probe_ref.shape[0]
    rows = words.shape[0] // big_sems.shape[0]
    small = [
        pltpu.make_async_copy(source, target, small_sems.at[i])
        for i, (source, target) in enumerate(
            ((probe_hbm, probe_ref), (scale_hbm, scale_ref), (mean_hbm, mean_ref))
        )
    ]
    big = [
        pltpu.make_async_copy(
            words_hbm.at[pl.ds(g * rows, rows)], words.at[pl.ds(g * rows, rows)], big_sems.at[g]
        )
        for g in range(big_sems.shape[0])
    ]
    for copy in small + big:
        copy.start()
    for copy in small:
        copy.wait()
    weight = probe_ref[...].astype(F32) * scale_ref[...]
    high = weight.astype(BF16)
    both_parts = jnp.concatenate([high.astype(F32), weight - high.astype(F32)], axis=0).astype(BF16)
    shift = jnp.sum(weight * mean_ref[...], axis=1, keepdims=True)
    for g, copy in enumerate(big):
        copy.wait()
        packed = words[g * rows : (g + 1) * rows, :]
        for p in range(4):
            digits = jnp.bitwise_and(packed, 3 << (2 * p)).astype(F32).astype(BF16)
            first = (4 * g + p) * rows
            digits_ref[first : first + rows, :] = digits
            both = lax.dot_general(both_parts, digits, NT, preferred_element_type=F32)
            total = (both[0:rank, :] + both[rank : 2 * rank, :]) * (0.25**p) - shift
            for q in range(rows // LANES):
                chunk = total[:, q * LANES : (q + 1) * LANES]
                out_ref[first // LANES + q] = chunk.astype(BF16)


def sketch_partial(genotype, probe, mean, scale, pieces):
    words, snps = genotype.shape
    rank = probe.shape[0]
    operands = [
        pltpu.with_memory_space_constraint(x, pltpu.HBM) for x in (genotype, probe, mean, scale)
    ]
    return pl.pallas_call(
        sketch_kernel,
        in_specs=[HBM] * 4,
        out_specs=[VMEM] * 4,
        out_shape=[
            pltpu.VMEM((4 * words // LANES, rank, LANES), BF16),
            pltpu.VMEM((4 * words, snps), BF16),
            pltpu.VMEM((1, snps), F32),
            pltpu.VMEM((1, snps), F32),
        ],
        scratch_shapes=[
            pltpu.VMEM((words, snps), jnp.int32),
            pltpu.VMEM((rank, snps), BF16),
            pltpu.SemaphoreType.DMA((3,)),
            pltpu.SemaphoreType.DMA((pieces,)),
        ],
        compiler_params=params(16),
        name="sketch",
    )(*operands)


def gather_kernel(parts_ref, out_ref):
    total = parts_ref[0].astype(F32)
    for source in range(1, parts_ref.shape[0]):
        total = total + parts_ref[source].astype(F32)
    chunk = total.astype(BF16)
    for target in range(out_ref.shape[0]):
        out_ref[target] = chunk


def sum_and_copy(parts):
    return pl.pallas_call(
        gather_kernel,
        in_specs=[VMEM],
        out_specs=VMEM,
        out_shape=jax.ShapeDtypeStruct(parts.shape, BF16),
        compiler_params=params(4),
        name="sumsnp",
    )(parts)


def project_kernel(pieces, digits_ref, sketch_ref, mean_ref, scale_ref, out_ref):
    chunks, rank, width = sketch_ref.shape
    blocks = [sketch_ref[b].astype(F32) for b in range(chunks)]
    plane = [(b * 4 * pieces // chunks) % 4 for b in range(chunks)]
    left = jnp.concatenate([blocks[b] * (0.25 ** plane[b]) for b in range(chunks)], axis=1)
    total = jnp.dot(left.astype(BF16), digits_ref[...], preferred_element_type=F32)
    sketch = jnp.concatenate(blocks, axis=1)
    sums = jnp.sum(sketch, axis=1, keepdims=True)
    sketch = sketch.astype(BF16)
    gram = lax.dot_general(sketch, sketch, NT, preferred_element_type=F32)
    high = gram.astype(BF16).astype(F32)
    side = jnp.concatenate(
        [jnp.zeros((rank, HALF), F32), high, gram - high, jnp.zeros((rank, HALF - 2 * rank), F32)],
        axis=1,
    )
    low = lax.broadcasted_iota(jnp.int32, (rank, width), 1) < HALF
    for c in range(total.shape[1] // width):
        cols = slice(c * width, (c + 1) * width)
        block = (total[:, cols] - mean_ref[:, cols] * sums) * scale_ref[:, cols]
        out_ref[2 * c] = jnp.where(low, block, side).astype(BF16)
        out_ref[2 * c + 1] = jnp.where(low, pltpu.roll(block, HALF, 1), side).astype(BF16)


def project_partial(digits, sketch, mean, scale, pieces):
    snps = digits.shape[1]
    _, rank, width = sketch.shape
    return pl.pallas_call(
        functools.partial(project_kernel, pieces),
        in_specs=[VMEM] * 4,
        out_specs=VMEM,
        out_shape=jax.ShapeDtypeStruct((snps // HALF, rank, width), BF16),
        compiler_params=params(8),
        name="project",
    )(digits, sketch, mean, scale)


def solve_kernel(parts_ref, out_ref):
    sources, rank, width = parts_ref.shape
    work = parts_ref[0].astype(F32)
    for source in range(1, sources):
        work = work + parts_ref[source].astype(F32)
    lane = lax.broadcasted_iota(jnp.int32, (rank, width), 1)
    low_part = pltpu.roll(work, width - rank, 1)
    work = jnp.where(lane < HALF, work, work + low_part)
    row = lax.broadcasted_iota(jnp.int32, (rank, 1), 0)
    scales = jnp.zeros((rank, 1), F32)
    for k in range(rank):
        pivot_row = work[k : k + 1, :]
        column = work[:, HALF + k : HALF + k + 1]
        pivot = work[k : k + 1, HALF + k : HALF + k + 1]
        scales = jnp.where(row == k, lax.rsqrt(pivot), scales)
        factor = jnp.where(row > k, column / pivot, 0.0)
        work = work - factor * pivot_row
    work = work * scales
    first = jnp.where(lane[0:8] < HALF, work[0:8], pltpu.roll(work[8:16], HALF, 1))
    chunk = jnp.concatenate([first, work[16:24]], axis=0).astype(BF16)
    for target in range(out_ref.shape[0]):
        out_ref[target] = chunk


def solve(parts):
    sources, _, width = parts.shape
    return pl.pallas_call(
        solve_kernel,
        in_specs=[VMEM],
        out_specs=VMEM,
        out_shape=jax.ShapeDtypeStruct((sources, 16, width), BF16),
        compiler_params=params(4),
        name="solve",
    )(parts)


def finish_kernel(parts_ref, out_ref):
    chunks, _, width = parts_ref.shape
    low = lax.broadcasted_iota(jnp.int32, (8, width), 1) < HALF
    for c in range(chunks // 2):
        cols = slice(c * width, (c + 1) * width)
        even, odd = parts_ref[2 * c].astype(F32), parts_ref[2 * c + 1].astype(F32)
        even_turned, odd_turned = pltpu.roll(even, HALF, 1), pltpu.roll(odd, HALF, 1)
        out_ref[0:8, cols] = jnp.where(low, even[0:8], odd_turned[0:8])
        out_ref[8:16, cols] = jnp.where(low, even_turned[0:8], odd[0:8])
        out_ref[16:24, cols] = jnp.where(low, even[8:16], odd_turned[8:16])


def finish(parts, rank):
    chunks, _, width = parts.shape
    return pl.pallas_call(
        finish_kernel,
        in_specs=[VMEM],
        out_specs=VMEM,
        out_shape=jax.ShapeDtypeStruct((rank, chunks * width // 2), F32),
        compiler_params=params(4),
        name="finish",
    )(parts)


def exchange(chunks, axis):
    return lax.all_to_all(chunks, axis, 0, 0, tiled=True)


def on_device(genotype, probe, allele_mean, allele_scale):
    mean, scale = allele_mean[None, :], allele_scale[None, :]
    pieces = max(1, genotype.shape[0] // 256)
    parts, digits, mean, scale = sketch_partial(genotype, probe, mean, scale, pieces)
    sketch = exchange(sum_and_copy(exchange(parts, "snp")), "snp")
    parts = exchange(project_partial(digits, sketch, mean, scale, pieces), "ind")
    return finish(exchange(solve(parts), "ind"), probe.shape[0])


def solution(mesh):
    in_specs = (P("ind", "snp"), P(None, "snp"), P("snp"), P("snp"))
    return jax.shard_map(
        on_device, mesh=mesh, in_specs=in_specs, out_specs=P(None, "snp"), check_vma=False
    )
```

time: 553 us -> 73.8 us (0.13)
  waiting for transfers between devices: 263 us -> 0 us
  other arithmetic: 153 us -> 0 us
  blocking collectives: 98 us -> 64.4 us
  between operations: 13.5 us -> 0.03 us
  local copies, waits for them, and re-layouts: 11.2 us -> 0 us
  matrix products: 9.34 us -> 0 us
  Pallas kernels: 0 us -> 9.14 us
    psum x2 -> x0, waiting for transfers between devices: 263 us -> none  [the longest x1 146 us: on_device(): return lax.psum(product.astype(jnp.bfloat16), 'ind').astype(jnp.float32)]
    convert_element_type x34 -> x0, other arithmetic: 108 us -> none  [the longest x32 106 us: unpack(): ((codes.astype(jnp.float32) - allele_mean) * allele_scale).astype(jnp.bfl...]
    psum x1 -> x0, blocking collectives: 98 us -> none  [on_device(): total = lax.psum(gram, ('ind', 'snp'))]
    all_to_all x0 -> x4, blocking collectives: none -> 64.4 us  [exchange(): return lax.all_to_all(chunks, axis, 0, 0, tiled=True)]
    another operation x37 -> x0, other arithmetic: 44.5 us -> none  [the longest x32 39.1 us: unpack(): stacked = jnp.stack(planes, axis=1)]
    pallas_call x0 -> x5, Pallas kernels: none -> 9.14 us  [the longest x1 4.52 us: sketch_partial(): pl.pallas_call(sketch_kernel, in_specs=[HBM] * 4, out_specs=[VMEM] * 4, o...]
    dot_general x33 -> x0, matrix products: 8.14 us -> none  [the longest x16 4.13 us: one_block(): lax.dot_general(probe, zed, (((1,), (1,)), ((), ())), preferred_element_t...]
    while x1 -> x0, local copies, waits for them, and re-layouts: 6.58 us -> none  [sketch_rows(): pieces = lax.map(one_block, blocks)]
  transfers between devices with their start and end apart: 2 -> 0, of which waited for: 2 -> 0; matrix products, arithmetic and copies ran while one was open for 0% -> 0% of each run, Pallas kernels for 0% -> 0%
where the time goes in v2:
time: 73.8 us; the launch traced here: 73.6 us
  blocking collectives  64.4 us (87%)
  Pallas kernels  9.14 us (12%)
    all_to_all x4, blocking collectives, exchange(): return lax.all_to_all(chunks, axis, 0, 0, tiled=True)  64.4 us
    pallas_call x1, Pallas kernels, sketch_partial(): pl.pallas_call(sketch_kernel, in_specs=[HBM] * 4, out_specs=[VMEM] * 4, o...  4.52 us
    pallas_call x1, Pallas kernels, solve(): pl.pallas_call(solve_kernel, in_specs=[VMEM], out_specs=VMEM, out_shape=j...  2.13 us
    pallas_call x1, Pallas kernels, project_partial(): pl.pallas_call(functools.partial(project_kernel, pieces), in_specs=[VMEM]...  1.68 us

profile of v2, /device:TPU:1, one launch (start us, length us, event | category | flops | bytes accessed | tf_op | source)
XLA Modules:
  0.0 73.6 jit_solution(1693377289980503182)
XLA Ops:
  0.0 4.5 %sketch.1 = (bf16[16,24,128]{2,1,0:T(8,128)(2,1)S(1)}, bf16[2048,2048]{1,0:T(8,128)(2,1)S(1)}, f32[1,2048]{1,0:T(1,128)S(1)}, f32[1,2048]{1,0:T(1,128)S(1)}) custom-call(s32[512,2048]{1,0:T(8,128)} %words_hbm.1, bf16[24,2048]{1,0:T(8,128)(2,1)} %probe_hbm.1, f32[1,2048]{1,0:T(1,128)} %bitcast.2, f32[1,2048]{1,0:T(1,128)} %bitcast.3), custom_call_target="tpu_custom_call" | custom-call | tf_op jit(solution)/shard_map/sketch/pallas_call | solution.py:68
  4.5 17.7 %all_to_all.20.parts_ref = bf16[16,24,128]{2,1,0:T(8,128)(2,1)S(1)} all-to-all(bf16[16,24,128]{2,1,0:T(8,128)(2,1)S(1)} %get-tuple-element.10), channel_id=1, replica_groups=mesh['ind'=32,'snp'=16] {'snp'}, dimensions={0} | all-to-all | bytes 196608 | tf_op jit(solution)/shard_map/all_to_all | solution.py:206
  22.3 10.9 %all_to_all.21.sketch_ref = bf16[16,24,128]{2,1,0:T(8,128)(2,1)S(1)} all-to-all(bf16[16,24,128]{2,1,0:T(8,128)(2,1)S(1)} %sumsnp.1), channel_id=1, replica_groups=mesh['ind'=32,'snp'=16] {'snp'}, dimensions={0} | all-to-all | bytes 196608 | tf_op jit(solution)/shard_map/all_to_all | solution.py:206
  33.1 1.7 %project.1 = bf16[32,24,128]{2,1,0:T(8,128)(2,1)S(1)} custom-call(bf16[2048,2048]{1,0:T(8,128)(2,1)S(1)} %get-tuple-element.9.digits_ref, bf16[16,24,128]{2,1,0:T(8,128)(2,1)S(1)} %all_to_all.21.sketch_ref, f32[1,2048]{1,0:T(1,128)S(1)} %get-tuple-element.11.mean_ref, f32[1,2048]{1,0:T(1,128)S(1)} %get-tuple-element.12.scale_ref), custom_call_target="tpu_custom_call" | custom-call | tf_op jit(solution)/shard_map/project/pallas_call | solution.py:135
  34.8 22.5 %all_to_all.22.parts_ref = bf16[32,24,128]{2,1,0:T(8,128)(2,1)S(1)} all-to-all(bf16[32,24,128]{2,1,0:T(8,128)(2,1)S(1)} %project.1), channel_id=1, replica_groups=mesh['ind'=32,'snp'=16] {'ind'}, dimensions={0} | all-to-all | bytes 393216 | tf_op jit(solution)/shard_map/all_to_all | solution.py:206
  57.4 2.1 %solve.1 = bf16[32,16,128]{2,1,0:T(8,128)(2,1)S(1)} custom-call(bf16[32,24,128]{2,1,0:T(8,128)(2,1)S(1)} %all_to_all.22.parts_ref), custom_call_target="tpu_custom_call" | custom-call | tf_op jit(solution)/shard_map/solve/pallas_call | solution.py:171
  59.5 13.3 %all_to_all.23.parts_ref = bf16[32,16,128]{2,1,0:T(8,128)(2,1)S(1)} all-to-all(bf16[32,16,128]{2,1,0:T(8,128)(2,1)S(1)} %solve.1), channel_id=1, replica_groups=mesh['ind'=32,'snp'=16] {'ind'}, dimensions={0} | all-to-all | bytes 262144 | tf_op jit(solution)/shard_map/all_to_all | solution.py:206
  72.8 0.8 %finish.1 = f32[24,2048]{1,0:T(8,128)} custom-call(bf16[32,16,128]{2,1,0:T(8,128)(2,1)S(1)} %all_to_all.23.parts_ref), custom_call_target="tpu_custom_call" | custom-call | tf_op jit(solution)/shard_map/finish/pallas_call | solution.py:195
  (1 shorter events, 0.0 us)

commit v3 on v2

--- a/solution.py
+++ b/solution.py
@@ -7,7 +7,7 @@
 from jax.experimental.pallas import tpu as pltpu
 from jax.sharding import PartitionSpec as P
 
-F32, BF16 = jnp.float32, jnp.bfloat16
+F32, BF16, F8 = jnp.float32, jnp.bfloat16, jnp.float8_e4m3fn
 NT = (((1,), (1,)), ((), ()))
 LANES = 128
 HALF = 64
@@ -17,6 +17,15 @@
 
 def params(mib):
     return pltpu.CompilerParams(vmem_limit_bytes=mib << 20)
+
+
+def eighths(values, count):
+    pieces = []
+    for _ in range(count):
+        piece = values.astype(F8).astype(F32)
+        pieces.append(piece)
+        values = (values - piece) * 16.0
+    return jnp.concatenate(pieces, axis=0).astype(F8)
 
 
 def sketch_kernel(
@@ -42,8 +51,7 @@
     for copy in small:
         copy.wait()
     weight = probe_ref[...].astype(F32) * scale_ref[...]
-    high = weight.astype(BF16)
-    both_parts = jnp.concatenate([high.astype(F32), weight - high.astype(F32)], axis=0).astype(BF16)
+    pieces = eighths(weight * 4096.0, 3)
     shift = jnp.sum(weight * mean_ref[...], axis=1, keepdims=True)
     for g, copy in enumerate(big):
         copy.wait()
@@ -51,9 +59,12 @@
         for p in range(4):
             digits = jnp.bitwise_and(packed, 3 << (2 * p)).astype(F32).astype(BF16)
             first = (4 * g + p) * rows
-            digits_ref[first : first + rows, :] = digits
-            both = lax.dot_general(both_parts, digits, NT, preferred_element_type=F32)
-            total = (both[0:rank, :] + both[rank : 2 * rank, :]) * (0.25**p) - shift
+            for c in range(digits_ref.shape[0]):
+                digits_ref[c, first : first + rows, :] = digits[:, c * LANES : (c + 1) * LANES]
+            parts = lax.dot_general(pieces, digits.astype(F8), NT, preferred_element_type=F32)
+            parts = parts * (0.25**p / 4096.0)
+            total = parts[2 * rank : 3 * rank, :] * 2.0**-8 + parts[rank : 2 * rank, :] * 2.0**-4
+            total = total + parts[0:rank, :] - shift
             for q in range(rows // LANES):
                 chunk = total[:, q * LANES : (q + 1) * LANES]
                 out_ref[first // LANES + q] = chunk.astype(BF16)
@@ -71,7 +82,7 @@
         out_specs=[VMEM] * 4,
         out_shape=[
             pltpu.VMEM((4 * words // LANES, rank, LANES), BF16),
-            pltpu.VMEM((4 * words, snps), BF16),
+            pltpu.VMEM((snps // LANES, 4 * words, LANES), BF16),
             pltpu.VMEM((1, snps), F32),
             pltpu.VMEM((1, snps), F32),
         ],
@@ -86,24 +97,54 @@
     )(*operands)
 
 
+def chip_kernel(parts_ref, out_ref):
+    half = out_ref.shape[1]
+    first = lax.rem(lax.axis_index("snp"), 2) * half
+    for q in range(half):
+        ours = parts_ref[first + q].astype(F32) + parts_ref[2 * half + first + q].astype(F32)
+        chunk = ours.astype(BF16)
+        for target in range(out_ref.shape[0]):
+            out_ref[target, q] = chunk
+
+
+def sum_on_chip(parts, chips):
+    chunks, rank, width = parts.shape
+    return pl.pallas_call(
+        chip_kernel,
+        in_specs=[VMEM],
+        out_specs=VMEM,
+        out_shape=pltpu.VMEM((chips, chunks // 4, rank, width), BF16),
+        compiler_params=params(4),
+        name="sumchip",
+    )(parts)
+
+
 def gather_kernel(parts_ref, out_ref):
-    total = parts_ref[0].astype(F32)
-    for source in range(1, parts_ref.shape[0]):
-        total = total + parts_ref[source].astype(F32)
-    chunk = total.astype(BF16)
-    for target in range(out_ref.shape[0]):
-        out_ref[target] = chunk
-
-
-def sum_and_copy(parts):
+    for q in range(out_ref.shape[0]):
+        total = parts_ref[0, q].astype(F32)
+        for source in range(1, parts_ref.shape[0]):
+            total = total + parts_ref[source, q].astype(F32)
+        out_ref[q] = total.astype(BF16)
+
+
+def sum_over_chips(parts):
     return pl.pallas_call(
         gather_kernel,
         in_specs=[VMEM],
         out_specs=VMEM,
-        out_shape=jax.ShapeDtypeStruct(parts.shape, BF16),
+        out_shape=pltpu.VMEM(parts.shape[1:], BF16),
         compiler_params=params(4),
         name="sumsnp",
     )(parts)
+
+
+def sum_over_snps(parts, size):
+    pairs = [[i, i + 1] for i in range(0, size, 2)]
+    rings = [list(range(core, size, 2)) for core in range(2)]
+    both = lax.all_gather(parts, "snp", axis_index_groups=pairs, tiled=True)
+    parts = sum_on_chip(both, size // 2)
+    parts = lax.all_to_all(parts, "snp", 0, 0, axis_index_groups=rings, tiled=True)
+    return lax.all_gather(sum_over_chips(parts), "snp", axis_index_groups=pairs, tiled=True)
 
 
 def project_kernel(pieces, digits_ref, sketch_ref, mean_ref, scale_ref, out_ref):
@@ -111,7 +152,7 @@
     blocks = [sketch_ref[b].astype(F32) for b in range(chunks)]
     plane = [(b * 4 * pieces // chunks) % 4 for b in range(chunks)]
     left = jnp.concatenate([blocks[b] * (0.25 ** plane[b]) for b in range(chunks)], axis=1)
-    total = jnp.dot(left.astype(BF16), digits_ref[...], preferred_element_type=F32)
+    left = left.astype(BF16)
     sketch = jnp.concatenate(blocks, axis=1)
     sums = jnp.sum(sketch, axis=1, keepdims=True)
     sketch = sketch.astype(BF16)
@@ -122,15 +163,16 @@
         axis=1,
     )
     low = lax.broadcasted_iota(jnp.int32, (rank, width), 1) < HALF
-    for c in range(total.shape[1] // width):
+    for c in range(digits_ref.shape[0]):
         cols = slice(c * width, (c + 1) * width)
-        block = (total[:, cols] - mean_ref[:, cols] * sums) * scale_ref[:, cols]
+        total = jnp.dot(left, digits_ref[c], preferred_element_type=F32)
+        block = (total - mean_ref[:, cols] * sums) * scale_ref[:, cols]
         out_ref[2 * c] = jnp.where(low, block, side).astype(BF16)
         out_ref[2 * c + 1] = jnp.where(low, pltpu.roll(block, HALF, 1), side).astype(BF16)
 
 
 def project_partial(digits, sketch, mean, scale, pieces):
-    snps = digits.shape[1]
+    snps = digits.shape[0] * digits.shape[2]
     _, rank, width = sketch.shape
     return pl.pallas_call(
         functools.partial(project_kernel, pieces),
@@ -140,6 +182,38 @@
         compiler_params=params(8),
         name="project",
     )(digits, sketch, mean, scale)
+
+
+def eliminate(work, rank):
+    tiles = range(rank // 8)
+    rows = [work[8 * t : 8 * t + 8, :] for t in tiles]
+    columns = [
+        {
+            t: jnp.broadcast_to(rows[t][:, HALF + j : HALF + j + 1], (8, LANES))
+            for t in tiles
+            if t >= j // 8
+        }
+        for j in range(rank)
+    ]
+    sublane = lax.broadcasted_iota(jnp.int32, (8, LANES), 0)
+    scales = [jnp.zeros((8, LANES), F32) for _ in tiles]
+    for k in range(rank):
+        own, at = divmod(k, 8)
+        pivot = jnp.broadcast_to(columns[k][own][at : at + 1, :], (8, LANES))
+        scales[own] = jnp.where(sublane == at, lax.rsqrt(pivot), scales[own])
+        inverse = 1.0 / pivot
+        factors = {t: columns[k][t] * inverse for t in tiles if t >= own}
+        factors[own] = jnp.where(sublane > at, factors[own], 0.0)
+        for j in range(k + 1, rank):
+            entry = columns[k][j // 8][j % 8 : j % 8 + 1, :]
+            for t in tiles:
+                if t >= j // 8:
+                    columns[j][t] = columns[j][t] - factors[t] * entry
+        pivot_row = rows[own][at : at + 1, :]
+        for t in tiles:
+            if t >= own:
+                rows[t] = rows[t] - factors[t] * pivot_row
+    return [rows[t] * scales[t] for t in tiles]
 
 
 def solve_kernel(parts_ref, out_ref):
@@ -150,18 +224,9 @@
     lane = lax.broadcasted_iota(jnp.int32, (rank, width), 1)
     low_part = pltpu.roll(work, width - rank, 1)
     work = jnp.where(lane < HALF, work, work + low_part)
-    row = lax.broadcasted_iota(jnp.int32, (rank, 1), 0)
-    scales = jnp.zeros((rank, 1), F32)
-    for k in range(rank):
-        pivot_row = work[k : k + 1, :]
-        column = work[:, HALF + k : HALF + k + 1]
-        pivot = work[k : k + 1, HALF + k : HALF + k + 1]
-        scales = jnp.where(row == k, lax.rsqrt(pivot), scales)
-        factor = jnp.where(row > k, column / pivot, 0.0)
-        work = work - factor * pivot_row
-    work = work * scales
-    first = jnp.where(lane[0:8] < HALF, work[0:8], pltpu.roll(work[8:16], HALF, 1))
-    chunk = jnp.concatenate([first, work[16:24]], axis=0).astype(BF16)
+    done = eliminate(work, rank)
+    first = jnp.where(lane[0:8] < HALF, done[0], pltpu.roll(done[1], HALF, 1))
+    chunk = jnp.concatenate([first, done[2]], axis=0).astype(BF16)
     for target in range(out_ref.shape[0]):
         out_ref[target] = chunk
 
@@ -210,7 +275,7 @@
     mean, scale = allele_mean[None, :], allele_scale[None, :]
     pieces = max(1, genotype.shape[0] // 256)
     parts, digits, mean, scale = sketch_partial(genotype, probe, mean, scale, pieces)
-    sketch = exchange(sum_and_copy(exchange(parts, "snp")), "snp")
+    sketch = sum_over_snps(parts, lax.axis_size("snp"))
     parts = exchange(project_partial(digits, sketch, mean, scale, pieces), "ind")
     return finish(exchange(solve(parts), "ind"), probe.shape[0])
 

time: 73.8 us -> 70.5 us (0.955)
  Pallas kernels: 9.14 us -> 6.52 us
  blocking collectives: 64.4 us -> 63.4 us
    all_to_all x4 -> x2, blocking collectives: 64.4 us -> 35.4 us  [exchange(): return lax.all_to_all(chunks, axis, 0, 0, tiled=True)]
    all_to_all x0 -> x1, blocking collectives: none -> 17.5 us  [sum_over_snps(): lax.all_to_all(parts, 'snp', 0, 0, axis_index_groups=rings, tiled=True)]
    all_gather x0 -> x2, blocking collectives: none -> 10.4 us  [the longest x1 8.43 us: sum_over_snps(): both = lax.all_gather(parts, 'snp', axis_index_groups=pairs, tiled=True)]
    pallas_call x1, Pallas kernels: 2.13 us -> 0.56 us  [solve(): pl.pallas_call(solve_kernel, in_specs=[VMEM], out_specs=VMEM, out_shape=j...]
    pallas_call x1, Pallas kernels: 4.52 us -> 3.75 us  [sketch_partial(): pl.pallas_call(sketch_kernel, in_specs=[HBM] * 4, out_specs=[VMEM] * 4, o...]
where the time goes in v3:
time: 70.5 us; the launch traced here: 69.9 us
  blocking collectives  63.4 us (90%)
  Pallas kernels  6.52 us (9%)
    all_to_all x2, blocking collectives, exchange(): return lax.all_to_all(chunks, axis, 0, 0, tiled=True)  35.4 us
    all_to_all x1, blocking collectives, sum_over_snps(): lax.all_to_all(parts, 'snp', 0, 0, axis_index_groups=rings, tiled=True)  17.5 us
    all_gather x1, blocking collectives, sum_over_snps(): both = lax.all_gather(parts, 'snp', axis_index_groups=pairs, tiled=True)  8.43 us
    pallas_call x1, Pallas kernels, sketch_partial(): pl.pallas_call(sketch_kernel, in_specs=[HBM] * 4, out_specs=[VMEM] * 4, o...  3.75 us
    all_gather x1, blocking collectives, sum_over_snps(): lax.all_gather(sum_over_chips(parts), 'snp', axis_index_groups=pairs, til...  2.02 us

profile of v3, /device:TPU:1, one launch (start us, length us, event | category | flops | bytes accessed | tf_op | source)
XLA Modules:
  0.0 69.9 jit_solution(18284435510867212946)
XLA Ops:
  0.0 3.8 %sketch.1 = (bf16[16,24,128]{2,1,0:T(8,128)(2,1)S(1)}, bf16[16,2048,128]{2,1,0:T(8,128)(2,1)S(1)}, f32[1,2048]{1,0:T(1,128)S(1)}, f32[1,2048]{1,0:T(1,128)S(1)}) custom-call(s32[512,2048]{1,0:T(8,128)} %words_hbm.1, bf16[24,2048]{1,0:T(8,128)(2,1)} %probe_hbm.1, f32[1,2048]{1,0:T(1,128)} %bitcast.2, f32[1,2048]{1,0:T(1,128)} %bitcast.3), custom_call_target="tpu_custom_call" | custom-call | tf_op jit(solution)/shard_map/sketch/pallas_call | solution.py:79
  3.8 8.4 %all_gather.6.parts_ref = bf16[32,24,128]{2,1,0:T(8,128)(2,1)S(1)} all-gather(bf16[16,24,128]{2,1,0:T(8,128)(2,1)S(1)} %get-tuple-element.10), channel_id=1, replica_groups={{0,1},{2,3},{4,5},{6,7},{8,9},{10,11},{12,13},{14,15},{16,17},{18,19},{..., dimensions={0}, use_global_device_ids=true | all-gather | bytes 294912 | tf_op jit(solution)/shard_map/all_gather | solution.py:144
  12.2 17.5 %all_to_all.15.parts_ref = bf16[8,8,24,128]{3,2,1,0:T(8,128)(2,1)S(1)} all-to-all(bf16[8,8,24,128]{3,2,1,0:T(8,128)(2,1)S(1)} %sumchip.1), channel_id=1, replica_groups={{0,2,4,6,8,10,12,14},{1,3,5,7,9,11,13,15},{16,18,20,22,24,26,28,30},{17..., dimensions={0} | all-to-all | bytes 786432 | tf_op jit(solution)/shard_map/all_to_all | solution.py:146
  29.8 0.1 sumsnp.1
  29.8 2.0 %all_gather.7.sketch_ref = bf16[16,24,128]{2,1,0:T(8,128)(2,1)S(1)} all-gather(bf16[8,24,128]{2,1,0:T(8,128)(2,1)S(1)} %sumsnp.1), channel_id=1, replica_groups={{0,1},{2,3},{4,5},{6,7},{8,9},{10,11},{12,13},{14,15},{16,17},{18,19},{..., dimensions={0}, use_global_device_ids=true | all-gather | bytes 147456 | tf_op jit(solution)/shard_map/all_gather | solution.py:147
  31.8 1.3 %project.1 = bf16[32,24,128]{2,1,0:T(8,128)(2,1)S(1)} custom-call(bf16[16,2048,128]{2,1,0:T(8,128)(2,1)S(1)} %get-tuple-element.9.digits_ref, bf16[16,24,128]{2,1,0:T(8,128)(2,1)S(1)} %all_gather.7.sketch_ref, f32[1,2048]{1,0:T(1,128)S(1)} %get-tuple-element.11.mean_ref, f32[1,2048]{1,0:T(1,128)S(1)} %get-tuple-element.12.scale_ref), custom_call_target="tpu_custom_call" | custom-call | tf_op jit(solution)/shard_map/project/pallas_call | solution.py:177
  33.2 22.1 %all_to_all.16.parts_ref = bf16[32,24,128]{2,1,0:T(8,128)(2,1)S(1)} all-to-all(bf16[32,24,128]{2,1,0:T(8,128)(2,1)S(1)} %project.1), channel_id=1, replica_groups=mesh['ind'=32,'snp'=16] {'ind'}, dimensions={0} | all-to-all | bytes 393216 | tf_op jit(solution)/shard_map/all_to_all | solution.py:271
  55.3 0.6 solve.1
  55.9 13.3 %all_to_all.17.parts_ref = bf16[32,16,128]{2,1,0:T(8,128)(2,1)S(1)} all-to-all(bf16[32,16,128]{2,1,0:T(8,128)(2,1)S(1)} %solve.1), channel_id=1, replica_groups=mesh['ind'=32,'snp'=16] {'ind'}, dimensions={0} | all-to-all | bytes 262144 | tf_op jit(solution)/shard_map/all_to_all | solution.py:271
  69.2 0.8 %finish.1 = f32[24,2048]{1,0:T(8,128)} custom-call(bf16[32,16,128]{2,1,0:T(8,128)(2,1)S(1)} %all_to_all.17.parts_ref), custom_call_target="tpu_custom_call" | custom-call | tf_op jit(solution)/shard_map/finish/pallas_call | solution.py:260
  (1 shorter events, 0.0 us)

commit v4 on v3

--- a/solution.py
+++ b/solution.py
@@ -147,7 +147,15 @@
     return lax.all_gather(sum_over_chips(parts), "snp", axis_index_groups=pairs, tiled=True)
 
 
-def project_kernel(pieces, digits_ref, sketch_ref, mean_ref, scale_ref, out_ref):
+def power_below(top):
+    return jnp.floor(jnp.log2(32000.0 / jnp.maximum(top, 1e-30)))
+
+
+def blocks_of(rank):
+    return [(j, t) for j in range(rank // 8) for t in range(j, rank // 8)]
+
+
+def project_kernel(pieces, digits_ref, sketch_ref, mean_ref, scale_ref, out_ref, product_ref):
     chunks, rank, width = sketch_ref.shape
     blocks = [sketch_ref[b].astype(F32) for b in range(chunks)]
     plane = [(b * 4 * pieces // chunks) % 4 for b in range(chunks)]
@@ -157,18 +165,33 @@
     sums = jnp.sum(sketch, axis=1, keepdims=True)
     sketch = sketch.astype(BF16)
     gram = lax.dot_general(sketch, sketch, NT, preferred_element_type=F32)
-    high = gram.astype(BF16).astype(F32)
-    side = jnp.concatenate(
-        [jnp.zeros((rank, HALF), F32), high, gram - high, jnp.zeros((rank, HALF - 2 * rank), F32)],
-        axis=1,
-    )
-    low = lax.broadcasted_iota(jnp.int32, (rank, width), 1) < HALF
+    top = jnp.zeros((rank, width), F32)
     for c in range(digits_ref.shape[0]):
         cols = slice(c * width, (c + 1) * width)
         total = jnp.dot(left, digits_ref[c], preferred_element_type=F32)
         block = (total - mean_ref[:, cols] * sums) * scale_ref[:, cols]
-        out_ref[2 * c] = jnp.where(low, block, side).astype(BF16)
-        out_ref[2 * c + 1] = jnp.where(low, pltpu.roll(block, HALF, 1), side).astype(BF16)
+        product_ref[:, cols] = block
+        top = jnp.maximum(top, jnp.abs(block))
+    power = power_below(jnp.max(top, axis=1, keepdims=True))
+    gram_power = power_below(jnp.max(jnp.max(jnp.abs(gram), axis=1, keepdims=True), axis=0, keepdims=True))
+    gram = gram * jnp.exp2(gram_power)
+    sides = [gram[8 * t : 8 * t + 8, 8 * j : 8 * j + 8] for j, t in blocks_of(rank)]
+    sides += [power[0:8], power[8:16], power[16:24], jnp.broadcast_to(gram_power, (8, 1))]
+    used = 8 * len(blocks_of(rank)) + 4
+    side = jnp.concatenate(
+        [jnp.zeros((8, HALF), F32)] + sides + [jnp.zeros((8, HALF - used), F32)], axis=1
+    )
+    low = lax.broadcasted_iota(jnp.int32, (8, width), 1) < HALF
+    factor = jnp.broadcast_to(jnp.exp2(power), (rank, width))
+    for c in range(digits_ref.shape[0]):
+        block = product_ref[:, c * width : (c + 1) * width] * factor
+        tiles = [block[0:8], block[8:16], block[16:24]]
+        turned = [pltpu.roll(tile, HALF, 1) for tile in tiles]
+        even = [jnp.where(low, tiles[0], turned[1]), jnp.where(low, tiles[2], side)]
+        odd = [jnp.where(low, turned[0], tiles[1]), jnp.where(low, turned[2], side)]
+        for i, pair in enumerate((even, odd)):
+            whole = jnp.round(jnp.concatenate(pair, axis=0)).astype(jnp.int32)
+            out_ref[2 * c + i] = whole.astype(jnp.int16)
 
 
 def project_partial(digits, sketch, mean, scale, pieces):
@@ -178,33 +201,26 @@
         functools.partial(project_kernel, pieces),
         in_specs=[VMEM] * 4,
         out_specs=VMEM,
-        out_shape=jax.ShapeDtypeStruct((snps // HALF, rank, width), BF16),
+        out_shape=pltpu.VMEM((snps // HALF, 16, width), jnp.int16),
+        scratch_shapes=[pltpu.VMEM((rank, snps), F32)],
         compiler_params=params(8),
         name="project",
     )(digits, sketch, mean, scale)
 
 
-def eliminate(work, rank):
-    tiles = range(rank // 8)
-    rows = [work[8 * t : 8 * t + 8, :] for t in tiles]
-    columns = [
-        {
-            t: jnp.broadcast_to(rows[t][:, HALF + j : HALF + j + 1], (8, LANES))
-            for t in tiles
-            if t >= j // 8
-        }
-        for j in range(rank)
-    ]
+def eliminate(rows, columns):
+    tiles = range(len(rows))
+    rows = list(rows)
     sublane = lax.broadcasted_iota(jnp.int32, (8, LANES), 0)
     scales = [jnp.zeros((8, LANES), F32) for _ in tiles]
-    for k in range(rank):
+    for k in range(len(columns)):
         own, at = divmod(k, 8)
         pivot = jnp.broadcast_to(columns[k][own][at : at + 1, :], (8, LANES))
         scales[own] = jnp.where(sublane == at, lax.rsqrt(pivot), scales[own])
         inverse = 1.0 / pivot
         factors = {t: columns[k][t] * inverse for t in tiles if t >= own}
         factors[own] = jnp.where(sublane > at, factors[own], 0.0)
-        for j in range(k + 1, rank):
+        for j in range(k + 1, len(columns)):
             entry = columns[k][j // 8][j % 8 : j % 8 + 1, :]
             for t in tiles:
                 if t >= j // 8:
@@ -216,28 +232,39 @@
     return [rows[t] * scales[t] for t in tiles]
 
 
-def solve_kernel(parts_ref, out_ref):
-    sources, rank, width = parts_ref.shape
-    work = parts_ref[0].astype(F32)
-    for source in range(1, sources):
-        work = work + parts_ref[source].astype(F32)
-    lane = lax.broadcasted_iota(jnp.int32, (rank, width), 1)
-    low_part = pltpu.roll(work, width - rank, 1)
-    work = jnp.where(lane < HALF, work, work + low_part)
-    done = eliminate(work, rank)
-    first = jnp.where(lane[0:8] < HALF, done[0], pltpu.roll(done[1], HALF, 1))
+def lane_of(tile, lane):
+    return jnp.broadcast_to(tile[:, lane : lane + 1], tile.shape)
+
+
+def solve_kernel(rank, parts_ref, out_ref):
+    low = lax.broadcasted_iota(jnp.int32, (8, LANES), 1) < HALF
+    order = blocks_of(rank)
+    first_power = HALF + 8 * len(order)
+    upper = jnp.zeros((8, LANES), F32)
+    under = jnp.zeros((8, LANES), F32)
+    for source in range(parts_ref.shape[0]):
+        whole = parts_ref[source].astype(jnp.int32).astype(F32)
+        inverse = jnp.exp2(-whole[8:16])
+        steps = [lane_of(inverse, first_power + i) for i in range(4)]
+        upper = upper + whole[0:8] * jnp.where(low, steps[0], steps[1])
+        under = under + whole[8:16] * jnp.where(low, steps[2], steps[3])
+    columns = [
+        {t: lane_of(under, HALF + 8 * order.index((j // 8, t)) + j % 8) for t in range(j // 8, rank // 8)}
+        for j in range(rank)
+    ]
+    done = eliminate([upper, pltpu.roll(upper, HALF, 1), under], columns)
+    first = jnp.where(low, done[0], pltpu.roll(done[1], HALF, 1))
     chunk = jnp.concatenate([first, done[2]], axis=0).astype(BF16)
     for target in range(out_ref.shape[0]):
         out_ref[target] = chunk
 
 
-def solve(parts):
-    sources, _, width = parts.shape
-    return pl.pallas_call(
-        solve_kernel,
+def solve(parts, rank):
+    return pl.pallas_call(
+        functools.partial(solve_kernel, rank),
         in_specs=[VMEM],
         out_specs=VMEM,
-        out_shape=jax.ShapeDtypeStruct((sources, 16, width), BF16),
+        out_shape=jax.ShapeDtypeStruct(parts.shape, BF16),
         compiler_params=params(4),
         name="solve",
     )(parts)
@@ -277,7 +304,7 @@
     parts, digits, mean, scale = sketch_partial(genotype, probe, mean, scale, pieces)
     sketch = sum_over_snps(parts, lax.axis_size("snp"))
     parts = exchange(project_partial(digits, sketch, mean, scale, pieces), "ind")
-    return finish(exchange(solve(parts), "ind"), probe.shape[0])
+    return finish(exchange(solve(parts, probe.shape[0]), "ind"), probe.shape[0])
 
 
 def solution(mesh):

time: 70.5 us -> 69.3 us (0.983)
  blocking collectives: 63.4 us -> 61.9 us
    all_to_all x2, blocking collectives: 35.4 us -> 34 us  [exchange(): return lax.all_to_all(chunks, axis, 0, 0, tiled=True)]
where the time goes in v4:
time: 69.3 us; the launch traced here: 68.7 us
  blocking collectives  61.9 us (89%)
  Pallas kernels  6.76 us (10%)
    all_to_all x2, blocking collectives, exchange(): return lax.all_to_all(chunks, axis, 0, 0, tiled=True)  34 us
    all_to_all x1, blocking collectives, sum_over_snps(): lax.all_to_all(parts, 'snp', 0, 0, axis_index_groups=rings, tiled=True)  17.5 us
    all_gather x1, blocking collectives, sum_over_snps(): both = lax.all_gather(parts, 'snp', axis_index_groups=pairs, tiled=True)  8.43 us
    pallas_call x1, Pallas kernels, sketch_partial(): pl.pallas_call(sketch_kernel, in_specs=[HBM] * 4, out_specs=[VMEM] * 4, o...  3.75 us
    all_gather x1, blocking collectives, sum_over_snps(): lax.all_gather(sum_over_chips(parts), 'snp', axis_index_groups=pairs, til...  2.02 us
    pallas_call x1, Pallas kernels, project_partial(): pl.pallas_call(functools.partial(project_kernel, pieces), in_specs=[VMEM]...  1.48 us

profile of v4, /device:TPU:1, one launch (start us, length us, event | category | flops | bytes accessed | tf_op | source)
XLA Modules:
  0.0 68.7 jit_solution(13542115765701760306)
XLA Ops:
  0.0 3.8 %sketch.1 = (bf16[16,24,128]{2,1,0:T(8,128)(2,1)S(1)}, bf16[16,2048,128]{2,1,0:T(8,128)(2,1)S(1)}, f32[1,2048]{1,0:T(1,128)S(1)}, f32[1,2048]{1,0:T(1,128)S(1)}) custom-call(s32[512,2048]{1,0:T(8,128)} %words_hbm.1, bf16[24,2048]{1,0:T(8,128)(2,1)} %probe_hbm.1, f32[1,2048]{1,0:T(1,128)} %bitcast.2, f32[1,2048]{1,0:T(1,128)} %bitcast.3), custom_call_target="tpu_custom_call" | custom-call | tf_op jit(solution)/shard_map/sketch/pallas_call | solution.py:79
  3.8 8.4 %all_gather.6.parts_ref = bf16[32,24,128]{2,1,0:T(8,128)(2,1)S(1)} all-gather(bf16[16,24,128]{2,1,0:T(8,128)(2,1)S(1)} %get-tuple-element.10), channel_id=1, replica_groups={{0,1},{2,3},{4,5},{6,7},{8,9},{10,11},{12,13},{14,15},{16,17},{18,19},{..., dimensions={0}, use_global_device_ids=true | all-gather | bytes 294912 | tf_op jit(solution)/shard_map/all_gather | solution.py:144
  12.2 17.5 %all_to_all.15.parts_ref = bf16[8,8,24,128]{3,2,1,0:T(8,128)(2,1)S(1)} all-to-all(bf16[8,8,24,128]{3,2,1,0:T(8,128)(2,1)S(1)} %sumchip.1), channel_id=1, replica_groups={{0,2,4,6,8,10,12,14},{1,3,5,7,9,11,13,15},{16,18,20,22,24,26,28,30},{17..., dimensions={0} | all-to-all | bytes 786432 | tf_op jit(solution)/shard_map/all_to_all | solution.py:146
  29.8 0.1 sumsnp.1
  29.8 2.0 %all_gather.7.sketch_ref = bf16[16,24,128]{2,1,0:T(8,128)(2,1)S(1)} all-gather(bf16[8,24,128]{2,1,0:T(8,128)(2,1)S(1)} %sumsnp.1), channel_id=1, replica_groups={{0,1},{2,3},{4,5},{6,7},{8,9},{10,11},{12,13},{14,15},{16,17},{18,19},{..., dimensions={0}, use_global_device_ids=true | all-gather | bytes 147456 | tf_op jit(solution)/shard_map/all_gather | solution.py:147
  31.8 1.5 %project.1 = s16[32,16,128]{2,1,0:T(8,128)(2,1)S(1)} custom-call(bf16[16,2048,128]{2,1,0:T(8,128)(2,1)S(1)} %get-tuple-element.9.digits_ref, bf16[16,24,128]{2,1,0:T(8,128)(2,1)S(1)} %all_gather.7.sketch_ref, f32[1,2048]{1,0:T(1,128)S(1)} %get-tuple-element.11.mean_ref, f32[1,2048]{1,0:T(1,128)S(1)} %get-tuple-element.12.scale_ref), custom_call_target="tpu_custom_call" | custom-call | tf_op jit(solution)/shard_map/project/pallas_call | solution.py:200
  33.3 20.9 %all_to_all.16.parts_ref = s16[32,16,128]{2,1,0:T(8,128)(2,1)S(1)} all-to-all(s16[32,16,128]{2,1,0:T(8,128)(2,1)S(1)} %project.1), channel_id=1, replica_groups=mesh['ind'=32,'snp'=16] {'ind'}, dimensions={0} | all-to-all | bytes 262144 | tf_op jit(solution)/shard_map/all_to_all | solution.py:298
  54.2 0.7 solve.1
  54.9 13.0 %all_to_all.17.parts_ref = bf16[32,16,128]{2,1,0:T(8,128)(2,1)S(1)} all-to-all(bf16[32,16,128]{2,1,0:T(8,128)(2,1)S(1)} %solve.1), channel_id=1, replica_groups=mesh['ind'=32,'snp'=16] {'ind'}, dimensions={0} | all-to-all | bytes 262144 | tf_op jit(solution)/shard_map/all_to_all | solution.py:298
  68.0 0.8 %finish.1 = f32[24,2048]{1,0:T(8,128)} custom-call(bf16[32,16,128]{2,1,0:T(8,128)(2,1)S(1)} %all_to_all.17.parts_ref), custom_call_target="tpu_custom_call" | custom-call | tf_op jit(solution)/shard_map/finish/pallas_call | solution.py:287
  (1 shorter events, 0.0 us)

commit v5 on v4

--- a/solution.py
+++ b/solution.py
@@ -7,7 +7,7 @@
 from jax.experimental.pallas import tpu as pltpu
 from jax.sharding import PartitionSpec as P
 
-F32, BF16, F8 = jnp.float32, jnp.bfloat16, jnp.float8_e4m3fn
+F32, BF16 = jnp.float32, jnp.bfloat16
 NT = (((1,), (1,)), ((), ()))
 LANES = 128
 HALF = 64
@@ -17,15 +17,6 @@
 
 def params(mib):
     return pltpu.CompilerParams(vmem_limit_bytes=mib << 20)
-
-
-def eighths(values, count):
-    pieces = []
-    for _ in range(count):
-        piece = values.astype(F8).astype(F32)
-        pieces.append(piece)
-        values = (values - piece) * 16.0
-    return jnp.concatenate(pieces, axis=0).astype(F8)
 
 
 def sketch_kernel(
@@ -51,7 +42,8 @@
     for copy in small:
         copy.wait()
     weight = probe_ref[...].astype(F32) * scale_ref[...]
-    pieces = eighths(weight * 4096.0, 3)
+    high = weight.astype(BF16)
+    both_parts = jnp.concatenate([high.astype(F32), weight - high.astype(F32)], axis=0).astype(BF16)
     shift = jnp.sum(weight * mean_ref[...], axis=1, keepdims=True)
     for g, copy in enumerate(big):
         copy.wait()
@@ -61,10 +53,8 @@
             first = (4 * g + p) * rows
             for c in range(digits_ref.shape[0]):
                 digits_ref[c, first : first + rows, :] = digits[:, c * LANES : (c + 1) * LANES]
-            parts = lax.dot_general(pieces, digits.astype(F8), NT, preferred_element_type=F32)
-            parts = parts * (0.25**p / 4096.0)
-            total = parts[2 * rank : 3 * rank, :] * 2.0**-8 + parts[rank : 2 * rank, :] * 2.0**-4
-            total = total + parts[0:rank, :] - shift
+            both = lax.dot_general(both_parts, digits, NT, preferred_element_type=F32)
+            total = (both[0:rank, :] + both[rank : 2 * rank, :]) * (0.25**p) - shift
             for q in range(rows // LANES):
                 chunk = total[:, q * LANES : (q + 1) * LANES]
                 out_ref[first // LANES + q] = chunk.astype(BF16)

time: 69.3 us -> 70 us (1.010)
  Pallas kernels: 6.76 us -> 7.48 us
    pallas_call x1, Pallas kernels: 3.75 us -> 4.47 us  [sketch_partial(): pl.pallas_call(sketch_kernel, in_specs=[HBM] * 4, out_specs=[VMEM] * 4, o...]
where the time goes in v5:
time: 70 us; the launch traced here: 69.4 us
  blocking collectives  61.9 us (88%)
  Pallas kernels  7.48 us (11%)
    all_to_all x2, blocking collectives, exchange(): return lax.all_to_all(chunks, axis, 0, 0, tiled=True)  34 us
    all_to_all x1, blocking collectives, sum_over_snps(): lax.all_to_all(parts, 'snp', 0, 0, axis_index_groups=rings, tiled=True)  17.5 us
    all_gather x1, blocking collectives, sum_over_snps(): both = lax.all_gather(parts, 'snp', axis_index_groups=pairs, tiled=True)  8.42 us
    pallas_call x1, Pallas kernels, sketch_partial(): pl.pallas_call(sketch_kernel, in_specs=[HBM] * 4, out_specs=[VMEM] * 4, o...  4.47 us
    all_gather x1, blocking collectives, sum_over_snps(): lax.all_gather(sum_over_chips(parts), 'snp', axis_index_groups=pairs, til...  2.02 us
    pallas_call x1, Pallas kernels, project_partial(): pl.pallas_call(functools.partial(project_kernel, pieces), in_specs=[VMEM]...  1.48 us

profile of v5, /device:TPU:1, one launch (start us, length us, event | category | flops | bytes accessed | tf_op | source)
XLA Modules:
  0.0 69.4 jit_solution(10523098106708514464)
XLA Ops:
  0.0 4.5 %sketch.1 = (bf16[16,24,128]{2,1,0:T(8,128)(2,1)S(1)}, bf16[16,2048,128]{2,1,0:T(8,128)(2,1)S(1)}, f32[1,2048]{1,0:T(1,128)S(1)}, f32[1,2048]{1,0:T(1,128)S(1)}) custom-call(s32[512,2048]{1,0:T(8,128)} %words_hbm.1, bf16[24,2048]{1,0:T(8,128)(2,1)} %probe_hbm.1, f32[1,2048]{1,0:T(1,128)} %bitcast.2, f32[1,2048]{1,0:T(1,128)} %bitcast.3), custom_call_target="tpu_custom_call" | custom-call | tf_op jit(solution)/shard_map/sketch/pallas_call | solution.py:69
  4.5 8.4 %all_gather.6.parts_ref = bf16[32,24,128]{2,1,0:T(8,128)(2,1)S(1)} all-gather(bf16[16,24,128]{2,1,0:T(8,128)(2,1)S(1)} %get-tuple-element.10), channel_id=1, replica_groups={{0,1},{2,3},{4,5},{6,7},{8,9},{10,11},{12,13},{14,15},{16,17},{18,19},{..., dimensions={0}, use_global_device_ids=true | all-gather | bytes 294912 | tf_op jit(solution)/shard_map/all_gather | solution.py:134
  12.9 17.5 %all_to_all.15.parts_ref = bf16[8,8,24,128]{3,2,1,0:T(8,128)(2,1)S(1)} all-to-all(bf16[8,8,24,128]{3,2,1,0:T(8,128)(2,1)S(1)} %sumchip.1), channel_id=1, replica_groups={{0,2,4,6,8,10,12,14},{1,3,5,7,9,11,13,15},{16,18,20,22,24,26,28,30},{17..., dimensions={0} | all-to-all | bytes 786432 | tf_op jit(solution)/shard_map/all_to_all | solution.py:136
  30.5 0.1 sumsnp.1
  30.5 2.0 %all_gather.7.sketch_ref = bf16[16,24,128]{2,1,0:T(8,128)(2,1)S(1)} all-gather(bf16[8,24,128]{2,1,0:T(8,128)(2,1)S(1)} %sumsnp.1), channel_id=1, replica_groups={{0,1},{2,3},{4,5},{6,7},{8,9},{10,11},{12,13},{14,15},{16,17},{18,19},{..., dimensions={0}, use_global_device_ids=true | all-gather | bytes 147456 | tf_op jit(solution)/shard_map/all_gather | solution.py:137
  32.6 1.5 %project.1 = s16[32,16,128]{2,1,0:T(8,128)(2,1)S(1)} custom-call(bf16[16,2048,128]{2,1,0:T(8,128)(2,1)S(1)} %get-tuple-element.9.digits_ref, bf16[16,24,128]{2,1,0:T(8,128)(2,1)S(1)} %all_gather.7.sketch_ref, f32[1,2048]{1,0:T(1,128)S(1)} %get-tuple-element.11.mean_ref, f32[1,2048]{1,0:T(1,128)S(1)} %get-tuple-element.12.scale_ref), custom_call_target="tpu_custom_call" | custom-call | tf_op jit(solution)/shard_map/project/pallas_call | solution.py:190
  34.0 20.9 %all_to_all.16.parts_ref = s16[32,16,128]{2,1,0:T(8,128)(2,1)S(1)} all-to-all(s16[32,16,128]{2,1,0:T(8,128)(2,1)S(1)} %project.1), channel_id=1, replica_groups=mesh['ind'=32,'snp'=16] {'ind'}, dimensions={0} | all-to-all | bytes 262144 | tf_op jit(solution)/shard_map/all_to_all | solution.py:288
  55.0 0.7 solve.1
  55.6 13.0 %all_to_all.17.parts_ref = bf16[32,16,128]{2,1,0:T(8,128)(2,1)S(1)} all-to-all(bf16[32,16,128]{2,1,0:T(8,128)(2,1)S(1)} %solve.1), channel_id=1, replica_groups=mesh['ind'=32,'snp'=16] {'ind'}, dimensions={0} | all-to-all | bytes 262144 | tf_op jit(solution)/shard_map/all_to_all | solution.py:288
  68.7 0.8 %finish.1 = f32[24,2048]{1,0:T(8,128)} custom-call(bf16[32,16,128]{2,1,0:T(8,128)(2,1)S(1)} %all_to_all.17.parts_ref), custom_call_target="tpu_custom_call" | custom-call | tf_op jit(solution)/shard_map/finish/pallas_call | solution.py:277
  (1 shorter events, 0.0 us)
